TPU v7x, 32 devices: a whole 2x2x4 slice. The times are simulated.
32 devices in a mesh: row: 4 (over x, core), col: 8 (over z, y).
Axes of the slice: x: 2, y: 2, z: 4, core: 2. Of those that a mesh axis runs over, the one named last changes fastest.
Arguments:
- hidden_in: bfloat16 [4, 8, 512, 896], P('row', 'col'), may hold values from -6 to 6
- targets: bfloat16 [4, 8, 512, 896], P('row', 'col'), may hold values from -6 to 6
- first_params: float32 [4, 896, 896], P('row', 'col'), may hold values from -0.1875 to 0.1875
- first_moment: float32 [4, 896, 896], P('row', 'col'), may hold values from -0.06 to 0.06
- second_params: float32 [8, 896, 896], P('col', 'row'), may hold values from -0.1875 to 0.1875
- second_moment: float32 [8, 896, 896], P('col', 'row'), may hold values from -0.06 to 0.06
Outputs:
- first_params_new: float32 [4, 896, 896], P('row', 'col')
- first_moment_new: float32 [4, 896, 896], P('row', 'col')
- second_params_new: float32 [8, 896, 896], P('col', 'row')
- second_moment_new: float32 [8, 896, 896], P('col', 'row')
All inputs are finite; a program needn't handle non-finite values.
Results may differ from a plain program's by a relative error of at most 0.022.
Values may be sent and summed in bfloat16 or wider, within the bound.
No kernel may reach another device: no remote copies, remote signals or barrier semaphores. Data moves between devices by JAX's collectives and lax.ppermute only.
A program may use at most 64 MiB of HBM per device.

v0:
```python
import jax
import jax.numpy as jnp
from jax import lax
from jax.sharding import PartitionSpec as P

outer_momentum = 0.9
outer_rate = 0.7


def passed_along(x, axis, by):
    length = lax.axis_size(axis)
    return lax.ppermute(x, axis, [(i, (i + by) % length) for i in range(length)])


def gelu_tanh(value):
    return jax.nn.gelu(value, approximate=True)


def nesterov(params, moment, grad):
    moment_new = outer_momentum * moment + grad
    return (params - outer_rate * (grad + outer_momentum * moment_new), moment_new)


def per_device(hidden_in, targets, first_params, first_moment, second_params, second_moment):
    inputs = hidden_in[0, 0]
    wanted = targets[0, 0]
    tokens = inputs.shape[0]
    offset = lax.axis_size("col") // 4
    pre = jnp.dot(
        inputs,
        lax.all_gather(first_params[0].astype(jnp.bfloat16), "col", axis=0, tiled=True),
        preferred_element_type=jnp.float32,
    )
    second_full = lax.all_gather(second_params[0].astype(jnp.bfloat16), "row", axis=0, tiled=True)
    active, slope = jax.vjp(gelu_tanh, pre)
    active_b = active.astype(jnp.bfloat16)
    output = jnp.dot(active_b, second_full, preferred_element_type=jnp.float32)
    error = ((output - wanted.astype(jnp.float32)) / tokens).astype(jnp.bfloat16)
    back = lax.dot_general(
        error, second_full, (((1,), (1,)), ((), ())), preferred_element_type=jnp.float32
    )
    grad_pre = slope(back)[0].astype(jnp.bfloat16)
    picked = active_b
    second_grad = lax.psum_scatter(
        lax.dot_general(
            picked, error, (((0,), (0,)), ((), ())), preferred_element_type=jnp.float32
        ).astype(jnp.bfloat16),
        "row",
        scatter_dimension=0,
        tiled=True,
    ).astype(jnp.float32) / lax.axis_size("row")
    picked = inputs
    first_grad = lax.psum_scatter(
        lax.dot_general(
            picked, grad_pre, (((0,), (0,)), ((), ())), preferred_element_type=jnp.float32
        ).astype(jnp.bfloat16),
        "col",
        scatter_dimension=0,
        tiled=True,
    ).astype(jnp.float32) / lax.axis_size("col")
    first_params_new, first_moment_new = nesterov(first_params, first_moment, first_grad[None])
    second_upd, second_mom = nesterov(second_params, second_moment, second_grad[None])
    stacked = jnp.stack([second_upd, second_mom])
    moved = passed_along(stacked.astype(jnp.bfloat16), "col", offset).astype(stacked.dtype)
    return (first_params_new, first_moment_new, moved[0], moved[1])


def solution(mesh):
    return jax.shard_map(
        per_device,
        mesh=mesh,
        in_specs=(
            P("row", "col", None, None),
            P("row", "col", None, None),
            P("row", "col", None),
            P("row", "col", None),
            P("col", "row", None),
            P("col", "row", None),
        ),
        out_specs=(
            P("row", "col", None),
            P("row", "col", None),
            P("col", "row", None),
            P("col", "row", None),
        ),
        check_vma=False,
    )
```

profile of v0, /device:TPU:0, one launch (start us, length us, event | category | flops | bytes accessed | tf_op | source)
XLA Modules:
  0.0 197.8 jit_solution(2901205608396926962)
XLA Ops:
  7.2 0.0 copy-start
  7.2 0.0 all-gather.5.cloned.1.call-start
  7.2 1.8 convert_element_type.54
  9.0 0.0 all-gather.5.cloned.1.call-update
  9.0 0.0 all-gather.7.cloned.1.call-start
  9.1 1.9 convert_element_type.57
  11.0 0.0 all-gather.7.cloned.1.call-update
  11.0 0.0 reduce-scatter.5.cloned.1.call-start
  11.1 47.0 %all-gather.5.cloned.1.call-done = bf16[1,896,896]{2,1,0:T(8,128)(2,1)} async-done(((bf16[1,112,896]{2,1,0:T(8,128)(2,1)}), bf16[1,896,896]{2,1,0:T(8,128)(2,1)}) %all-gather.5.cloned.1.call-update) | async-done | bytes 1605648 | tf_op jit(solution)/shard_map/all_gather | solution.py:31
  58.0 3.9 %fusion.13 = f32[512,896]{1,0:T(8,128)} fusion(bf16[1,896,896]{2,1,0:T(8,128)(2,1)} %all-gather.5.cloned.1.call-done, bf16[1,1,512,896]{3,2,1,0:T(8,128)(2,1)S(1)} %copy-done), kind=kOutput, calls=%fused_computation.19 | convolution fusion | flops 822083584 | bytes 4358144 | tf_op jit(solution)/shard_map/dot_general | solution.py:29
  61.9 16.5 %all-gather.7.cloned.1.call-done = bf16[1,896,896]{2,1,0:T(8,128)(2,1)} async-done(((bf16[1,224,896]{2,1,0:T(8,128)(2,1)}), bf16[1,896,896]{2,1,0:T(8,128)(2,1)}) %all-gather.7.cloned.1.call-update) | async-done | bytes 1605648 | tf_op jit(solution)/shard_map/all_gather | solution.py:34
  78.4 3.4 %fusion.8 = bf16[512,896]{1,0:T(8,128)(2,1)S(1)} fusion(bf16[1,896,896]{2,1,0:T(8,128)(2,1)} %all-gather.7.cloned.1.call-done, bf16[1,1,512,896]{3,2,1,0:T(8,128)(2,1)S(1)} %copy-done.5, f32[512,896]{1,0:T(8,128)} %fusion.13), kind=kOutput, calls=%fused_computation.11 | convolution fusion | flops 828047360 | bytes 5275648 | tf_op jit(solution)/shard_map/dot_general | solution.py:37
  81.8 1.0 copy-done.7
  82.8 2.4 %convolution_convert_fusion = bf16[896,896]{1,0:T(8,128)(2,1)} fusion(bf16[512,896]{1,0:T(8,128)(2,1)S(1)} %fusion.8, f32[512,896]{1,0:T(8,128)S(1)} %copy-done.6), kind=kOutput, calls=%fused_computation.13 | convolution fusion | flops 827015168 | bytes 4358144 | tf_op jit(solution)/shard_map/dot_general | solution.py:45
  85.2 0.0 reduce-scatter.5.cloned.1.call-update
  85.2 0.0 reduce-scatter.7.cloned.1.call-start
  85.2 4.9 %fusion.17 = bf16[896,896]{0,1:T(8,128)(2,1)S(1)} fusion(f32[512,896]{1,0:T(8,128)} %fusion.13, bf16[512,896]{1,0:T(8,128)(2,1)} %copy-done.7, bf16[1,896,896]{2,1,0:T(8,128)(2,1)} %all-gather.7.cloned.1.call-done, bf16[1,1,512,896]{3,2,1,0:T(8,128)(2,1)S(1)} %copy-done), kind=kOutput, calls=%fused_computation.21 | convolution fusion | flops 1654145024 | bytes 6881280 | tf_op jit(solution)/shard_map/dot_general | solution.py:54
  90.1 2.3 %copy.18 = bf16[896,896]{1,0:T(8,128)(2,1)} copy(bf16[896,896]{0,1:T(8,128)(2,1)S(1)} %fusion.17) | data formatting | bytes 3211264
  92.5 0.0 reduce-scatter.7.cloned.1.call-update
  92.5 21.0 %reduce-scatter.5.cloned.1.call-done = bf16[224,896]{1,0:T(8,128)(2,1)} async-done(((bf16[896,896]{1,0:T(8,128)(2,1)}), bf16[224,896]{1,0:T(8,128)(2,1)}) %reduce-scatter.5.cloned.1.call-update) | async-done | bytes 401424 | tf_op jit(solution)/shard_map/reduce_scatter | solution.py:44
  113.5 1.2 fusion.37
  114.8 1.0 pad_maximum_fusion
  115.8 1.5 collective-permute-start
  117.3 0.2 copy.15
  117.5 0.2 copy.14
  117.7 67.9 %reduce-scatter.7.cloned.1.call-done = bf16[112,896]{1,0:T(8,128)(2,1)} async-done(((bf16[896,896]{1,0:T(8,128)(2,1)}), bf16[112,896]{1,0:T(8,128)(2,1)}) %reduce-scatter.7.cloned.1.call-update) | async-done | bytes 200720
  185.6 1.1 copy.19
  186.7 0.1 bitcast_add_fusion.3
  186.9 0.9 copy.16
  187.8 0.9 copy.17
  188.7 1.2 convert_element_type.68
  190.0 1.3 slice_bitcast_fusion
  (15 shorter events, 0.0 us)
Async XLA Ops:
  7.2 50.9 %copy-start = (bf16[1,1,512,896]{3,2,1,0:T(8,128)(2,1)S(1)}, bf16[1,1,512,896]{3,2,1,0:T(8,128)(2,1)}, u32[]{:S(2)}) copy-start(bf16[1,1,512,896]{3,2,1,0:T(8,128)(2,1)} %param.6) | copy-start | bytes 2752516
  7.2 50.9 %all-gather.5.cloned.1.call-start = ((), (), s32[]{:S(2)}) async-start(), calls=%async_computation.3 | async-start | bytes 1806336 | tf_op jit(solution)/shard_map/all_gather | solution.py:31
  9.0 69.4 %all-gather.7.cloned.1.call-start = ((), (), s32[]{:S(2)}) async-start(), calls=%async_computation.4 | async-start | bytes 2007040 | tf_op jit(solution)/shard_map/all_gather | solution.py:34
  11.0 67.4 %copy-start.5 = (bf16[1,1,512,896]{3,2,1,0:T(8,128)(2,1)S(1)}, bf16[1,1,512,896]{3,2,1,0:T(8,128)(2,1)}, u32[]{:S(2)}) copy-start(bf16[1,1,512,896]{3,2,1,0:T(8,128)(2,1)} %param.7) | copy-start | bytes 2752516
  11.0 102.5 %reduce-scatter.5.cloned.1.call-start = ((), (), s32[]{:S(2)}) async-start(), calls=%async_computation.2 | async-start | bytes 2007040 | tf_op jit(solution)/shard_map/reduce_scatter | solution.py:44
  78.4 4.4 %copy-start.6 = (f32[512,896]{1,0:T(8,128)S(1)}, f32[512,896]{1,0:T(8,128)}, u32[]{:S(2)}) copy-start(f32[512,896]{1,0:T(8,128)} %fusion.13) | copy-start | bytes 5505028
  81.8 1.0 copy-start.7
  85.2 100.4 %reduce-scatter.7.cloned.1.call-start = ((), (), s32[]{:S(2)}) async-start(), calls=%async_computation.5 | async-start | bytes 1806336
  90.1 23.4 %copy-start.1 = (f32[1,224,896]{2,1,0:T(8,128)S(1)}, f32[1,224,896]{2,1,0:T(8,128)}, u32[]{:S(2)}) copy-start(f32[1,224,896]{2,1,0:T(8,128)} %param.10) | copy-start | bytes 2408452
  92.5 21.1 %copy-start.3 = (f32[1,224,896]{2,1,0:T(8,128)S(1)}, f32[1,224,896]{2,1,0:T(8,128)}, u32[]{:S(2)}) copy-start(f32[1,224,896]{2,1,0:T(8,128)} %param.11) | copy-start | bytes 2408452
  92.5 24.8 %copy-start.2 = (f32[1,112,896]{2,1,0:T(8,128)S(1)}, f32[1,112,896]{2,1,0:T(8,128)}, u32[]{:S(2)}) copy-start(f32[1,112,896]{2,1,0:T(8,128)} %param.8) | copy-start | bytes 1204228
  114.8 2.7 %copy-start.4 = (f32[1,112,896]{2,1,0:T(8,128)S(1)}, f32[1,112,896]{2,1,0:T(8,128)}, u32[]{:S(2)}) copy-start(f32[1,112,896]{2,1,0:T(8,128)} %param.9) | copy-start | bytes 1204228
  115.8 73.0 %collective-permute-start = (bf16[2,1,224,896]{3,2,1,0:T(8,128)(2,1)}, bf16[2,1,224,896]{3,2,1,0:T(8,128)(2,1)}, u32[]{:S(2)}, u32[]{:S(2)}) collective-permute-start(bf16[2,1,224,896]{3,2,1,0:T(8,128)(2,1)} %pad_maximum_fusion), channel_id=1, source_target_pairs={{0,2},{1,3},{2,4},{3,5},{4,6},{5,7},{6,0},{7,1},{8,10},{9,11},{10,... | collective-permute-start | bytes 2408456 | tf_op jit(solution)/shard_map/ppermute | solution.py:12
Sparse Core Ops, SparseCore 0:
  10.7 47.2 all-gather.4
  60.2 18.1 all-gather.6
  85.3 28.1 reduce-scatter.4
  116.9 68.7 reduce-scatter.6
where the time goes:
time: 198 us
  waiting for transfers between devices  152 us (77%)
  matrix products  14.6 us (7%)
  between operations  13.9 us (7%)
  local copies, waits for them, and re-layouts  7.96 us (4%)
  other arithmetic  7.29 us (4%)
    unnamed x5, waiting for transfers between devices  68 us
    all_gather x1, waiting for transfers between devices, per_device(): lax.all_gather(first_params[0].astype(jnp.bfloat16), 'col', axis=0, tiled...  47 us
    reduce_scatter x1, waiting for transfers between devices, per_device(): lax.psum_scatter(lax.dot_general(picked, error, (((0,), (0,)), ((), ())),...  21 us
    all_gather x1, waiting for transfers between devices, per_device(): lax.all_gather(second_params[0].astype(jnp.bfloat16), 'row', axis=0, tile...  16.5 us
    unnamed x22, local copies, waits for them, and re-layouts  6.71 us
    dot_general x1, matrix products, per_device(): lax.dot_general(picked, grad_pre, (((0,), (0,)), ((), ())), preferred_ele...  4.88 us
  transfers between devices with their start and end apart: 5, of which 4 were waited for; matrix products, arithmetic and copies ran while one was open for 9% of the time, Pallas kernels for 0%

commit v1 on v0

--- a/solution.py
+++ b/solution.py
@@ -28,7 +28,15 @@
     offset = lax.axis_size("col") // 4
     pre = jnp.dot(
         inputs,
-        lax.all_gather(first_params[0].astype(jnp.bfloat16), "col", axis=0, tiled=True),
+        jnp.concatenate(
+            lax.all_to_all(
+                jnp.stack([first_params[0].astype(jnp.bfloat16)] * lax.axis_size("col")),
+                "col",
+                0,
+                0,
+            ),
+            axis=0,
+        ),
         preferred_element_type=jnp.float32,
     )
     second_full = lax.all_gather(second_params[0].astype(jnp.bfloat16), "row", axis=0, tiled=True)

time: 198 us -> 176 us (0.89)
  waiting for transfers between devices: 152 us -> 125 us
  starting transfers between devices: 1.66 us -> 9.06 us
    all_gather x1 -> x0, waiting for transfers between devices: 47 us -> none  [per_device(): lax.all_gather(first_params[0].astype(jnp.bfloat16), 'col', axis=0, tiled...]
    all_to_all x0 -> x1, waiting for transfers between devices: none -> 36.8 us  [per_device(): lax.all_to_all(jnp.stack([first_params[0].astype(jnp.bfloat16)] * lax.axi...]
    all_gather x1, waiting for transfers between devices: 16.5 us -> 0.01 us  [per_device(): lax.all_gather(second_params[0].astype(jnp.bfloat16), 'row', axis=0, tile...]
    all_to_all x0 -> x1, starting transfers between devices: none -> 7.44 us  [per_device(): lax.all_to_all(jnp.stack([first_params[0].astype(jnp.bfloat16)] * lax.axi...]
    unnamed x5 -> x4, waiting for transfers between devices: 68 us -> 68.1 us
    unnamed x22 -> x20, local copies, waits for them, and re-layouts: 6.71 us -> 6.69 us
  transfers between devices with their start and end apart: 5 -> 5, of which waited for: 4 -> 3; matrix products, arithmetic and copies ran while one was open for 9% -> 9% of each run, Pallas kernels for 0% -> 0%
where the time goes in v1:
time: 176 us
  waiting for transfers between devices  125 us (71%)
  between operations  13.9 us (8%)
  matrix products  13.4 us (8%)
  local copies, waits for them, and re-layouts  9.24 us (5%)
  starting transfers between devices  9.06 us (5%)
  other arithmetic  5.48 us (3%)
    unnamed x4, waiting for transfers between devices  68.1 us
    all_to_all x1, waiting for transfers between devices, per_device(): lax.all_to_all(jnp.stack([first_params[0].astype(jnp.bfloat16)] * lax.axi...  36.8 us
    reduce_scatter x1, waiting for transfers between devices, per_device(): lax.psum_scatter(lax.dot_general(picked, error, (((0,), (0,)), ((), ())),...  20.2 us
    all_to_all x1, starting transfers between devices, per_device(): lax.all_to_all(jnp.stack([first_params[0].astype(jnp.bfloat16)] * lax.axi...  7.44 us
    unnamed x20, local copies, waits for them, and re-layouts  6.69 us
    dot_general x1, matrix products, per_device(): lax.dot_general(picked, grad_pre, (((0,), (0,)), ((), ())), preferred_ele...  4.88 us
    dot_general x1, matrix products, per_device(): output = jnp.dot(active_b, second_full, preferred_element_type=jnp.float32)  3.64 us
  transfers between devices with their start and end apart: 5, of which 3 were waited for; matrix products, arithmetic and copies ran while one was open for 9% of the time, Pallas kernels for 0%

profile of v1, /device:TPU:0, one launch (start us, length us, event | category | flops | bytes accessed | tf_op | source)
XLA Modules:
  0.0 176.1 jit_solution(2760551912253480810)
XLA Ops:
  7.2 0.0 copy-start
  7.2 1.1 convert_bitcast_fusion
  8.3 1.3 stack.11
  9.6 7.4 %all-to-all-start = ((bf16[8,112,896]{2,1,0:T(8,128)(2,1)}), bf16[8,112,896]{2,1,0:T(8,128)(2,1)S(1)}, u32[]{:S(2)}, u32[]{:S(2)}) async-start(bf16[8,112,896]{2,1,0:T(8,128)(2,1)} %stack.11), calls=%async_computation | async-start | bytes 3211264 | tf_op jit(solution)/shard_map/all_to_all | solution.py:32
  17.0 0.0 all-gather.3.cloned.1.call-start
  17.1 0.8 convert_element_type.54
  17.9 0.0 all-gather.3.cloned.1.call-update
  17.9 0.0 reduce-scatter.5.cloned.1.call-start
  17.9 36.8 %all-to-all-done = bf16[8,112,896]{2,1,0:T(8,128)(2,1)S(1)} async-done(((bf16[8,112,896]{2,1,0:T(8,128)(2,1)}), bf16[8,112,896]{2,1,0:T(8,128)(2,1)S(1)}, u32[]{:S(2)}, u32[]{:S(2)}) %all-to-all-start) | async-done | bytes 1605664 | tf_op jit(solution)/shard_map/all_to_all | solution.py:32
  54.7 2.5 %fusion.21 = f32[512,896]{1,0:T(8,128)} fusion(bf16[896,896]{1,0:T(8,128)(2,1)S(1)} %bitcast.62, bf16[1,1,512,896]{3,2,1,0:T(8,128)(2,1)S(1)} %copy-done), kind=kOutput, calls=%fused_computation.21 | convolution fusion | flops 822083584 | bytes 4358144 | tf_op jit(solution)/shard_map/dot_general | solution.py:29
  57.2 3.6 %fusion.8 = bf16[512,896]{1,0:T(8,128)(2,1)S(1)} fusion(bf16[1,896,896]{2,1,0:T(8,128)(2,1)} %all-gather.3.cloned.1.call-done, bf16[1,1,512,896]{3,2,1,0:T(8,128)(2,1)} %param.7, f32[512,896]{1,0:T(8,128)} %fusion.21), kind=kOutput, calls=%fused_computation.11 | convolution fusion | flops 828047360 | bytes 5275648 | tf_op jit(solution)/shard_map/dot_general | solution.py:45
  60.9 1.0 copy-done.6
  61.8 2.4 %convolution_convert_fusion = bf16[896,896]{1,0:T(8,128)(2,1)} fusion(bf16[512,896]{1,0:T(8,128)(2,1)S(1)} %fusion.8, f32[512,896]{1,0:T(8,128)S(1)} %copy-done.5), kind=kOutput, calls=%fused_computation.13 | convolution fusion | flops 827015168 | bytes 4358144 | tf_op jit(solution)/shard_map/dot_general | solution.py:53
  64.2 0.0 reduce-scatter.5.cloned.1.call-update
  64.3 0.0 reduce-scatter.7.cloned.1.call-start
  64.3 4.9 %fusion.15 = bf16[896,896]{0,1:T(8,128)(2,1)S(1)} fusion(f32[512,896]{1,0:T(8,128)} %fusion.21, bf16[512,896]{1,0:T(8,128)(2,1)} %copy-done.6, bf16[1,896,896]{2,1,0:T(8,128)(2,1)} %all-gather.3.cloned.1.call-done, bf16[1,1,512,896]{3,2,1,0:T(8,128)(2,1)S(1)} %copy-done), kind=kOutput, calls=%fused_computation.19 | convolution fusion | flops 1654145024 | bytes 6881280 | tf_op jit(solution)/shard_map/dot_general | solution.py:62
  69.2 2.3 %copy.18 = bf16[896,896]{1,0:T(8,128)(2,1)} copy(bf16[896,896]{0,1:T(8,128)(2,1)S(1)} %fusion.15) | data formatting | bytes 3211264
  71.5 0.0 reduce-scatter.7.cloned.1.call-update
  71.6 0.0 copy-start.2
  71.6 20.2 %reduce-scatter.5.cloned.1.call-done = bf16[224,896]{1,0:T(8,128)(2,1)} async-done(((bf16[896,896]{1,0:T(8,128)(2,1)}), bf16[224,896]{1,0:T(8,128)(2,1)}) %reduce-scatter.5.cloned.1.call-update) | async-done | bytes 401424 | tf_op jit(solution)/shard_map/reduce_scatter | solution.py:52
  91.7 1.2 fusion.36
  93.0 1.0 pad_maximum_fusion
  94.0 1.5 collective-permute-start
  95.5 0.2 copy.15
  95.7 0.2 copy.14
  95.9 68.1 %reduce-scatter.7.cloned.1.call-done = bf16[112,896]{1,0:T(8,128)(2,1)} async-done(((bf16[896,896]{1,0:T(8,128)(2,1)}), bf16[112,896]{1,0:T(8,128)(2,1)}) %reduce-scatter.7.cloned.1.call-update) | async-done | bytes 200720
  164.0 1.1 copy.19
  165.1 0.1 bitcast_add_fusion.3
  165.2 0.9 copy.16
  166.1 0.9 copy.17
  167.1 1.2 convert_element_type.65
  168.3 1.3 slice_bitcast_fusion
  (13 shorter events, 0.0 us)
Async XLA Ops:
  7.2 47.6 %copy-start = (bf16[1,1,512,896]{3,2,1,0:T(8,128)(2,1)S(1)}, bf16[1,1,512,896]{3,2,1,0:T(8,128)(2,1)}, u32[]{:S(2)}) copy-start(bf16[1,1,512,896]{3,2,1,0:T(8,128)(2,1)} %param.6) | copy-start | bytes 2752516
  9.6 7.5 %copy-start.1 = (f32[1,224,896]{2,1,0:T(8,128)S(1)}, f32[1,224,896]{2,1,0:T(8,128)}, u32[]{:S(2)}) copy-start(f32[1,224,896]{2,1,0:T(8,128)} %param.10) | copy-start | bytes 2408452
  9.6 45.1 %all-to-all-start = ((bf16[8,112,896]{2,1,0:T(8,128)(2,1)}), bf16[8,112,896]{2,1,0:T(8,128)(2,1)S(1)}, u32[]{:S(2)}, u32[]{:S(2)}) async-start(bf16[8,112,896]{2,1,0:T(8,128)(2,1)} %stack.11), calls=%async_computation | async-start | bytes 3211264 | tf_op jit(solution)/shard_map/all_to_all | solution.py:32
  17.0 40.2 %all-gather.3.cloned.1.call-start = ((), (), s32[]{:S(2)}) async-start(), calls=%async_computation.4 | async-start | bytes 2007040 | tf_op jit(solution)/shard_map/all_gather | solution.py:42
  17.9 73.8 %reduce-scatter.5.cloned.1.call-start = ((), (), s32[]{:S(2)}) async-start(), calls=%async_computation.3 | async-start | bytes 2007040 | tf_op jit(solution)/shard_map/reduce_scatter | solution.py:52
  57.2 4.6 %copy-start.5 = (f32[512,896]{1,0:T(8,128)S(1)}, f32[512,896]{1,0:T(8,128)}, u32[]{:S(2)}) copy-start(f32[512,896]{1,0:T(8,128)} %fusion.21) | copy-start | bytes 5505028
  60.9 1.0 copy-start.6
  64.3 99.7 %reduce-scatter.7.cloned.1.call-start = ((), (), s32[]{:S(2)}) async-start(), calls=%async_computation.5 | async-start | bytes 1806336
  71.5 20.2 %copy-start.3 = (f32[1,224,896]{2,1,0:T(8,128)S(1)}, f32[1,224,896]{2,1,0:T(8,128)}, u32[]{:S(2)}) copy-start(f32[1,224,896]{2,1,0:T(8,128)} %param.11) | copy-start | bytes 2408452
  71.6 23.9 %copy-start.2 = (f32[1,112,896]{2,1,0:T(8,128)S(1)}, f32[1,112,896]{2,1,0:T(8,128)}, u32[]{:S(2)}) copy-start(f32[1,112,896]{2,1,0:T(8,128)} %param.8) | copy-start | bytes 1204228
  93.0 2.7 %copy-start.4 = (f32[1,112,896]{2,1,0:T(8,128)S(1)}, f32[1,112,896]{2,1,0:T(8,128)}, u32[]{:S(2)}) copy-start(f32[1,112,896]{2,1,0:T(8,128)} %param.9) | copy-start | bytes 1204228
  94.0 73.1 %collective-permute-start = (bf16[2,1,224,896]{3,2,1,0:T(8,128)(2,1)}, bf16[2,1,224,896]{3,2,1,0:T(8,128)(2,1)}, u32[]{:S(2)}, u32[]{:S(2)}) collective-permute-start(bf16[2,1,224,896]{3,2,1,0:T(8,128)(2,1)} %pad_maximum_fusion), channel_id=1, source_target_pairs={{0,2},{1,3},{2,4},{3,5},{4,6},{5,7},{6,0},{7,1},{8,10},{9,11},{10,... | collective-permute-start | bytes 2408456 | tf_op jit(solution)/shard_map/ppermute | solution.py:12
Sparse Core Ops, SparseCore 0:
  20.0 21.2 all-gather.2
  64.4 27.2 reduce-scatter.4
  95.2 68.7 reduce-scatter.6
